TPU v7x, 256 devices: a whole 4x4x8 slice. The times are simulated.
256 devices in a mesh: seq: 32 (over x, z_hi, core), tensor: 8 (over z_lo, y).
Axes of the slice: x: 4, y: 4, z: 8 (z_hi: 4, z_lo: 2; z = z_hi * 2 + z_lo), core: 2. Of those that a mesh axis runs over, the one named last changes fastest.
Arguments:
- keyval: bfloat16 [16384, 8192], P('seq', 'tensor'), may hold values from -6 to 6
- gating: bfloat16 [16384, 8192], P('seq', 'tensor'), may hold values from -6 to 6
- skip_gain: float32 [8192], P('tensor'), may hold values from -4 to 4
- filter_values: float32 [2, 64, 2, 32, 8192], P(None, None, None, 'seq', 'tensor'), may hold values from -12 to 12
- blocks: int32 [64, 64], P('tensor'), may hold values from 0 to 255, as said below
- out_weight: bfloat16 [8192, 8192], P('seq', 'tensor'), may hold values from -0.0625 to 0.0625
Outputs:
- mixed: bfloat16 [16384, 8192], P('seq', 'tensor')
Inputs may be any that keep to these rules, and one draw needn't show every extreme that they name: Each row names 64 different blocks.
All inputs are finite; a program needn't handle non-finite values.
Results may differ from a plain program's by a relative error of at most 0.0063.
Values may be sent and summed in bfloat16 or wider, within the bound.
A program may use at most 128 MiB of HBM per device.

v0:
```python
import math

import jax
import jax.numpy as jnp
from jax import lax
from jax.sharding import PartitionSpec as P

BLOCK = 64


HIGHEST = lax.Precision.HIGHEST


def tables(first_index, second_index, length):
    phase = first_index * second_index % length
    angle = 2.0 * math.pi / length * phase.astype(jnp.float32)
    return (jnp.cos(angle), jnp.sin(angle))


def rounded(value):
    return lax.optimization_barrier(value.astype(jnp.bfloat16)).astype(jnp.float32)


def whole_conv(signal_group, block_list, filter_group, cycle_size, tokens_local):
    seq_length = cycle_size * tokens_local
    unit = signal_group.shape[1]
    repeat = filter_group.shape[2]
    signal = signal_group.astype(jnp.float32).reshape(cycle_size, tokens_local, unit)
    cycle_index = jnp.arange(cycle_size, dtype=jnp.int32)
    local_index = jnp.arange(tokens_local, dtype=jnp.int32)
    cosine_cycle, sine_cycle = tables(cycle_index[:, None], cycle_index[None, :], cycle_size)
    first_real = jnp.einsum("pa,ajc->pjc", cosine_cycle, signal, precision=HIGHEST)
    first_imaginary = -jnp.einsum("pa,ajc->pjc", sine_cycle, signal, precision=HIGHEST)
    cosine_twist, sine_twist = tables(cycle_index[:, None], local_index[None, :], seq_length)
    cosine_twist = cosine_twist[:, :, None]
    sine_twist = sine_twist[:, :, None]
    twist_real = rounded(first_real * cosine_twist + first_imaginary * sine_twist)
    twist_imaginary = rounded(first_imaginary * cosine_twist - first_real * sine_twist)
    kept_rows = (
        block_list[:, None] * repeat + jnp.arange(repeat, dtype=jnp.int32)[None, :]
    ).reshape(-1)
    cosine_kept, sine_kept = tables(kept_rows[:, None], local_index[None, :], tokens_local)
    spectrum_real = jnp.einsum(
        "qj,pjc->pqc", cosine_kept, twist_real, precision=HIGHEST
    ) + jnp.einsum("qj,pjc->pqc", sine_kept, twist_imaginary, precision=HIGHEST)
    spectrum_imaginary = jnp.einsum(
        "qj,pjc->pqc", cosine_kept, twist_imaginary, precision=HIGHEST
    ) - jnp.einsum("qj,pjc->pqc", sine_kept, twist_real, precision=HIGHEST)
    filter_real = filter_group[0].reshape(-1, cycle_size, unit).transpose(1, 0, 2)
    filter_imaginary = filter_group[1].reshape(-1, cycle_size, unit).transpose(1, 0, 2)
    product_real = filter_real * spectrum_real - filter_imaginary * spectrum_imaginary
    product_imaginary = filter_real * spectrum_imaginary + filter_imaginary * spectrum_real
    back_real = jnp.einsum(
        "qj,pqc->pjc", cosine_kept, product_real, precision=HIGHEST
    ) - jnp.einsum("qj,pqc->pjc", sine_kept, product_imaginary, precision=HIGHEST)
    back_imaginary = jnp.einsum(
        "qj,pqc->pjc", sine_kept, product_real, precision=HIGHEST
    ) + jnp.einsum("qj,pqc->pjc", cosine_kept, product_imaginary, precision=HIGHEST)
    turned_real = rounded(back_real * cosine_twist - back_imaginary * sine_twist)
    turned_imaginary = rounded(back_real * sine_twist + back_imaginary * cosine_twist)
    convolved = (
        jnp.einsum("pa,pjc->ajc", cosine_cycle, turned_real, precision=HIGHEST)
        - jnp.einsum("pa,pjc->ajc", sine_cycle, turned_imaginary, precision=HIGHEST)
    ) / seq_length
    return convolved.astype(jnp.bfloat16).reshape(seq_length, unit)


def body(keyval, gating, skip_gain, filter_values, blocks, out_weight):
    cycle_size = lax.axis_size("seq")
    cycle_pos = lax.axis_index("seq")
    tokens_local, channels = keyval.shape
    seq_length = tokens_local * cycle_size
    repeat = BLOCK // cycle_size
    groups_local = blocks.shape[0]
    group_width = channels // groups_local
    whole_weight = lax.all_gather(out_weight, "seq", axis=0, tiled=True)
    narrow = channels // cycle_size
    unit = min(narrow, group_width)
    subgroups = narrow // unit
    columns = lax.all_to_all(keyval, "seq", split_axis=1, concat_axis=0, tiled=True)
    filter_cols = lax.all_to_all(filter_values, "seq", split_axis=4, concat_axis=3, tiled=True)
    sub_group = (cycle_pos * narrow + jnp.arange(subgroups, dtype=jnp.int32) * unit) // group_width
    match = sub_group[:, None, None] == jnp.arange(groups_local, dtype=jnp.int32)[None, :, None]
    sub_blocks = jnp.sum(jnp.where(match, blocks[None, :, :], 0), axis=1)
    sub_signal = columns.reshape(seq_length, subgroups, unit).transpose(1, 0, 2)
    sub_filters = filter_cols.reshape(
        2, filter_cols.shape[1], repeat, cycle_size, subgroups, unit
    ).transpose(4, 0, 1, 2, 3, 5)

    def sub_step(items):
        return whole_conv(items[0], items[1], items[2], cycle_size, tokens_local)

    done = lax.map(sub_step, (sub_signal, sub_blocks, sub_filters))
    done = done.transpose(1, 0, 2).reshape(seq_length, narrow)
    convolved = lax.all_to_all(done, "seq", split_axis=0, concat_axis=1, tiled=True)
    hidden = (
        gating.astype(jnp.float32)
        * (convolved.astype(jnp.float32) + skip_gain[None, :] * keyval.astype(jnp.float32))
    ).astype(jnp.bfloat16)
    full_hidden = lax.all_gather(hidden, "tensor", axis=1, tiled=True)
    mixed_rows = jnp.dot(full_hidden, whole_weight, preferred_element_type=jnp.float32)
    return mixed_rows.astype(jnp.bfloat16)


def solution(mesh):
    placed = (
        P("seq", "tensor"),
        P("seq", "tensor"),
        P("tensor"),
        P(None, None, None, "seq", "tensor"),
        P("tensor", None),
        P("seq", "tensor"),
    )
    return jax.shard_map(
        body, mesh=mesh, in_specs=placed, out_specs=P("seq", "tensor"), check_vma=False
    )
```

profile of v0, /device:TPU:33, one launch (start us, length us, event | category | flops | bytes accessed | tf_op | source)
XLA Modules:
  0.0 406.2 jit_solution(17398672774952115893)
XLA Ops:
  6.5 2.3 copy.54
  8.8 10.9 %all-to-all-start.1 = ((bf16[512,32,32]{0,2,1:T(8,128)(2,1)}), bf16[512,32,32]{0,2,1:T(8,128)(2,1)S(1)}, u32[]{:S(2)}, u32[]{:S(2)}) async-start(bf16[512,32,32]{0,2,1:T(8,128)(2,1)} %bitcast.3), calls=%async_computation.1 | async-start | bytes 2097152 | tf_op jit(solution)/shard_map/all_to_all | solution.py:80
  19.7 4.2 %copy.51 = f32[2,64,2,1,1024]{1,2,3,0,4:T(2,128)S(1)} copy(f32[2,64,2,1,1024]{4,3,2,1,0:T(1,128)} %param.9) | data formatting | bytes 2097152 | tf_op args[3]
  23.9 3.2 reshape.112
  27.2 21.8 %all-to-all-done.1 = bf16[512,32,32]{0,2,1:T(8,128)(2,1)S(1)} async-done(((bf16[512,32,32]{0,2,1:T(8,128)(2,1)}), bf16[512,32,32]{0,2,1:T(8,128)(2,1)S(1)}, u32[]{:S(2)}, u32[]{:S(2)}) %all-to-all-start.1) | async-done | bytes 1048608 | tf_op jit(solution)/shard_map/all_to_all | solution.py:80
  49.0 4.8 %all-to-all-start = ((f32[32,1,8192]{2,1,0:T(1,128)}), f32[32,1,8192]{2,1,0:T(1,128)S(1)}, u32[]{:S(2)}, u32[]{:S(2)}) async-start(f32[32,1,8192]{2,1,0:T(1,128)} %reshape.112), calls=%async_computation | async-start | bytes 2097152 | tf_op jit(solution)/shard_map/all_to_all | solution.py:81
  57.9 2.5 fusion.13
  60.3 3.3 fusion.17
  63.6 3.3 fusion.2
  66.9 16.2 %all-to-all-done = f32[32,1,8192]{2,1,0:T(1,128)S(1)} async-done(((f32[32,1,8192]{2,1,0:T(1,128)}), f32[32,1,8192]{2,1,0:T(1,128)S(1)}, u32[]{:S(2)}, u32[]{:S(2)}) %all-to-all-start) | async-done | bytes 1048608 | tf_op jit(solution)/shard_map/all_to_all | solution.py:81
  83.6 16.2 %reduce.2 = f32[32,8192]{1,0:T(8,128)S(1)} reduce(f32[32,1,8192]{2,1,0:T(1,128)S(1)} %all-to-all-done, f32[]{:T(128)} %broadcast.243), dimensions={1}, to_apply=%all_to_all.12.reduce_sub_computation | reduce | bytes 2097156 | tf_op jit(solution)/shard_map/all_to_all | solution.py:81
  103.0 2.1 copy.52
  112.4 2.1 copy.61
  114.5 4.0 fusion.22
  118.5 2.8 fusion.26
  121.3 2.8 fusion.32
  124.1 2.8 convolution_add_fusion
  126.9 3.7 fusion.5
  135.3 4.1 %all-to-all-start.2 = ((bf16[32,512,32]{1,2,0:T(8,128)(2,1)}), bf16[32,512,32]{1,2,0:T(8,128)(2,1)S(1)}, u32[]{:S(2)}, u32[]{:S(2)}) async-start(bf16[32,512,32]{1,2,0:T(8,128)(2,1)} %copy.66), calls=%async_computation.2 | async-start | bytes 2097152 | tf_op jit(solution)/shard_map/all_to_all | solution.py:95
  140.1 29.2 %all-to-all-done.2 = bf16[32,512,32]{1,2,0:T(8,128)(2,1)S(1)} async-done(((bf16[32,512,32]{1,2,0:T(8,128)(2,1)}), bf16[32,512,32]{1,2,0:T(8,128)(2,1)S(1)}, u32[]{:S(2)}, u32[]{:S(2)}) %all-to-all-start.2) | async-done | bytes 1048608 | tf_op jit(solution)/shard_map/all_to_all | solution.py:95
  169.3 2.7 fusion.1
  172.8 88.6 %all-gather.3.cloned.1.call-done = bf16[512,8192]{0,1:T(8,128)(2,1)} async-done(((bf16[512,1024]{0,1:T(8,128)(2,1)}), bf16[512,8192]{0,1:T(8,128)(2,1)}) %all-gather.3.cloned.1.call-update) | async-done | bytes 8388624 | tf_op jit(solution)/shard_map/all_gather | solution.py:100
  261.4 122.2 %all-gather.5.cloned.1.call-done = bf16[8192,1024]{1,0:T(8,128)(2,1)} async-done(((bf16[256,1024]{1,0:T(8,128)(2,1)}), bf16[8192,1024]{1,0:T(8,128)(2,1)}) %all-gather.5.cloned.1.call-update) | async-done | bytes 16777232 | tf_op jit(solution)/shard_map/all_gather | solution.py:76
  383.5 15.6 %convolution_convert_fusion = bf16[512,1024]{1,0:T(8,128)(2,1)} fusion(bf16[512,8192]{0,1:T(8,128)(2,1)} %all-gather.3.cloned.1.call-done, bf16[8192,1024]{1,0:T(8,128)(2,1)} %all-gather.5.cloned.1.call-done), kind=kOutput, calls=%fused_computation.10 | convolution fusion | flops 8590458880 | bytes 26214400 | tf_op jit(solution)/shard_map/dot_general | solution.py:101
  (33 shorter events, 21.1 us)
Async XLA Ops:
  8.8 40.2 %all-to-all-start.1 = ((bf16[512,32,32]{0,2,1:T(8,128)(2,1)}), bf16[512,32,32]{0,2,1:T(8,128)(2,1)S(1)}, u32[]{:S(2)}, u32[]{:S(2)}) async-start(bf16[512,32,32]{0,2,1:T(8,128)(2,1)} %bitcast.3), calls=%async_computation.1 | async-start | bytes 2097152 | tf_op jit(solution)/shard_map/all_to_all | solution.py:80
  23.9 3.2 copy-start.4
  49.0 34.1 %all-to-all-start = ((f32[32,1,8192]{2,1,0:T(1,128)}), f32[32,1,8192]{2,1,0:T(1,128)S(1)}, u32[]{:S(2)}, u32[]{:S(2)}) async-start(f32[32,1,8192]{2,1,0:T(1,128)} %reshape.112), calls=%async_computation | async-start | bytes 2097152 | tf_op jit(solution)/shard_map/all_to_all | solution.py:81
  57.8 5.8 %copy-start = (bf16[32,512,32]{1,0,2:T(8,128)(2,1)}, bf16[32,512,32]{1,0,2:T(8,128)(2,1)S(1)}, u32[]{:S(2)}) copy-start(bf16[32,512,32]{1,0,2:T(8,128)(2,1)S(1)} %get-tuple-element.22) | copy-start | bytes 3145732
  110.4 4.1 %copy-start.1 = (bf16[32,512,32]{1,0,2:T(8,128)(2,1)S(1)}, bf16[32,512,32]{1,0,2:T(8,128)(2,1)}, u32[]{:S(2)}) copy-start(bf16[32,512,32]{1,0,2:T(8,128)(2,1)} %copy-done) | copy-start | bytes 3145732
  133.8 5.8 %copy-start.2 = (bf16[512,1024]{1,0:T(8,128)(2,1)S(1)}, bf16[512,1024]{1,0:T(8,128)(2,1)}, u32[]{:S(2)}) copy-start(bf16[512,1024]{1,0:T(8,128)(2,1)} %param.7) | copy-start | bytes 3145732
  135.3 34.0 %copy-start.3 = (f32[1024]{0:T(1024)S(1)}, f32[1024]{0:T(1024)}, u32[]{:S(2)}) copy-start(f32[1024]{0:T(1024)} %param.8) | copy-start | bytes 12292
  135.3 34.0 %all-to-all-start.2 = ((bf16[32,512,32]{1,2,0:T(8,128)(2,1)}), bf16[32,512,32]{1,2,0:T(8,128)(2,1)S(1)}, u32[]{:S(2)}, u32[]{:S(2)}) async-start(bf16[32,512,32]{1,2,0:T(8,128)(2,1)} %copy.66), calls=%async_computation.2 | async-start | bytes 2097152 | tf_op jit(solution)/shard_map/all_to_all | solution.py:95
  139.5 121.9 %all-gather.3.cloned.1.call-start = ((), (), s32[]{:S(2)}) async-start(), calls=%async_computation.3 | async-start | bytes 9437184 | tf_op jit(solution)/shard_map/all_gather | solution.py:100
  172.0 211.5 %all-gather.5.cloned.1.call-start = ((), (), s32[]{:S(2)}) async-start(), calls=%async_computation.4 | async-start | bytes 17301504 | tf_op jit(solution)/shard_map/all_gather | solution.py:76
Sparse Core Ops, SparseCore 0:
  172.2 89.1 all-gather.2
  263.9 119.5 all-gather.4
where the time goes:
time: 410 us; the launch traced here: 406 us
  waiting for transfers between devices  279 us (68%)
  matrix products  47.4 us (12%)
  local copies, waits for them, and re-layouts  27.1 us (7%)
  starting transfers between devices  19.8 us (5%)
  other arithmetic  19.3 us (5%)
  between operations  13.8 us (3%)
    all_gather x1, waiting for transfers between devices, body(): whole_weight = lax.all_gather(out_weight, 'seq', axis=0, tiled=True)  122 us
    all_gather x1, waiting for transfers between devices, body(): full_hidden = lax.all_gather(hidden, 'tensor', axis=1, tiled=True)  88.6 us
    all_to_all x1, waiting for transfers between devices, body(): lax.all_to_all(done, 'seq', split_axis=0, concat_axis=1, tiled=True)  29.2 us
    all_to_all x1, waiting for transfers between devices, body(): lax.all_to_all(keyval, 'seq', split_axis=1, concat_axis=0, tiled=True)  21.8 us
    all_to_all x1, other arithmetic, body(): lax.all_to_all(filter_values, 'seq', split_axis=4, concat_axis=3, tiled=T...  16.2 us
    all_to_all x1, waiting for transfers between devices, body(): lax.all_to_all(filter_values, 'seq', split_axis=4, concat_axis=3, tiled=T...  16.2 us
    dot_general x1, matrix products, body(): jnp.dot(full_hidden, whole_weight, preferred_element_type=jnp.float32)  15.6 us
    unnamed x15, local copies, waits for them, and re-layouts  11.7 us
  transfers between devices with their start and end apart: 5, of which 5 were waited for; matrix products, arithmetic and copies ran while one was open for 5% of the time, Pallas kernels for 0%

commit v1 on v0

v1 whole, which is shorter than its diff:
```python
import functools
import math

import jax
import jax.numpy as jnp
from jax import lax
from jax.experimental import pallas as pl
from jax.experimental.pallas import tpu as pltpu
from jax.sharding import PartitionSpec as P

BLOCK = 64
SEQ = 32
OUTER = 8
INNER = 4
TOK = 512
QUARTER = 128
WIDTH = 1024
UNIT = 32
KEPT = 128
STEP = 16
ROWS = TOK // STEP
LENGTH = SEQ * TOK
F32 = jnp.float32
BF16 = jnp.bfloat16
MESH = pl.DeviceIdType.MESH


def iota(shape, axis):
    return lax.broadcasted_iota(jnp.int32, shape, axis)


def sine(x):
    s = x * x
    t = -1.0 / 39916800.0
    for c in (1.0 / 362880.0, -1.0 / 5040.0, 1.0 / 120.0, -1.0 / 6.0, 1.0):
        t = t * s + c
    return x * t


def cosine_of(phase):
    d = jnp.abs((phase & 511) - 256) - 128
    return sine(d.astype(F32) * (math.pi / 256.0))


def halves(v):
    hi = v.astype(BF16)
    return hi, (v - hi.astype(F32)).astype(BF16)


def dot(a, b):
    return jnp.dot(a, b, preferred_element_type=F32)


def turn(v, num, den, sign):
    re, im = v
    num = num % den
    if num == 0:
        return v
    if 4 * num == den:
        return (-im, re) if sign > 0 else (im, -re)
    c = math.cos(2 * math.pi * num / den)
    s = sign * math.sin(2 * math.pi * num / den)
    if 8 * num == den:
        h = c
        return (h * (re - im), h * (re + im)) if sign > 0 else (h * (re + im), h * (im - re))
    if 8 * num == 3 * den:
        h = -c
        return (-h * (re + im), h * (re - im)) if sign > 0 else (h * (im - re), -h * (re + im))
    return (re * c - im * s, re * s + im * c)


def transform(values, sign):
    n = len(values)
    if n == 1:
        return values
    even = transform(values[0::2], sign)
    odd = transform(values[1::2], sign)
    odd = [turn(o, k, n, sign) for k, o in enumerate(odd)]
    low = [(e[0] + o[0], e[1] + o[1]) for e, o in zip(even, odd)]
    high = [(e[0] - o[0], e[1] - o[1]) for e, o in zip(even, odd)]
    return low + high


def swap(parts, perm):
    u = dot(jnp.concatenate(parts, axis=1), perm[...]).astype(BF16)
    return [u[:, QUARTER * i : QUARTER * (i + 1)] for i in range(INNER)]


def kernel(
    tensor, kv, gate, skip, filt, kcol, krow, out,
    xs, xr, fs, fr, mh, ml, th, tl, dm, eh, el, perm, tw, rq, g, fst, fm, b, vh, vl, cs, cr, hid,
    xsend, xrecv, fsend, frecv, csend, crecv, gsend, grecv, local,
):
    me = lax.axis_index("seq")
    ten = lax.axis_index("tensor")
    zl, y = ten // 4, lax.rem(ten, 4)
    far = (1 - zl) * 4
    zp = far + y
    up, down = lax.rem(y + 1, 4), lax.rem(y + 3, 4)
    yp, ym = zl * 4 + up, zl * 4 + down

    barrier = pltpu.get_barrier_semaphore()

    @pl.loop(1, SEQ)
    def _(i):
        pl.semaphore_signal(
            barrier, inc=1, device_id={"seq": lax.rem(me + i, SEQ)}, device_id_type=MESH
        )

    if tensor:
        for t in (zp, yp, ym):
            pl.semaphore_signal(barrier, inc=1, device_id={"tensor": t}, device_id_type=MESH)

    @pl.loop(0, 8)
    def _(r):
        i = iota((64, 512), 0) + r * 64
        n = iota((64, 512), 1)
        same = ((i >> 7) == ((n >> 5) & 3)) & (((i >> 5) & 3) == (n >> 7)) & ((i & 31) == (n & 31))
        perm[pl.ds(pl.multiple_of(r * 64, 64), 64), :] = jnp.where(same, 1.0, 0.0).astype(BF16)

    def remote(src, dst, ss, rs, dev, axis="seq"):
        return pltpu.make_async_remote_copy(
            src_ref=src, dst_ref=dst, send_sem=ss, recv_sem=rs,
            device_id={axis: dev}, device_id_type=MESH,
        )

    def lanes(i):
        return pl.ds(pl.multiple_of(i * QUARTER, QUARTER), QUARTER)

    def deliver(dest, part, staged, landed, ss, rs):
        staged[dest] = part

        @pl.when(dest != me)
        def _():
            remote(staged.at[dest], landed.at[me], ss.at[dest], rs.at[me], dest).start()

        @pl.when(dest == me)
        def _():
            landed[me] = part

    def collect(landed, staged, ss, rs):
        @pl.loop(1, SEQ)
        def _(i):
            src = lax.rem(me + i, SEQ)
            remote(staged.at[src], landed.at[src], ss.at[src], rs.at[src], src).wait_recv()

    def settle(landed, staged, ss, rs):
        @pl.loop(1, SEQ)
        def _(i):
            src = lax.rem(me + i, SEQ)
            remote(staged.at[src], landed.at[src], ss.at[src], rs.at[src], src).wait_send()

    pl.semaphore_wait(barrier, SEQ - 1 + (3 if tensor else 0))

    @pl.loop(0, OUTER)
    def _(i):
        tile = lax.rem(me // INNER + i, OUTER)
        parts = [kv[QUARTER * k : QUARTER * (k + 1), lanes(tile)] for k in range(INNER)]
        for q, part in enumerate(swap(parts, perm)):
            deliver(tile * INNER + q, part, xs, xr, xsend, xrecv)

    @pl.loop(0, OUTER)
    def _(i):
        tile = lax.rem(me // INNER + i, OUTER)
        parts = []
        for k in range(INNER):
            pair = [
                filt[pl.ds(m * 1024 + 256 * k + tile, UNIT, stride=8), :].astype(BF16)
                for m in range(2)
            ]
            parts.append(jnp.concatenate(pair, axis=0))
        for q, part in enumerate(swap(parts, perm)):
            deliver(tile * INNER + q, part, fs, fr, fsend, frecv)

    @pl.loop(0, KEPT // STEP)
    def _(r):
        rows = pl.ds(pl.multiple_of(r * STEP, STEP), STEP)
        more = pl.ds(pl.multiple_of(r * STEP + KEPT, STEP), STEP)
        phase = kcol[rows, 0:1] * iota((STEP, TOK), 1)
        ch, cl = halves(cosine_of(phase))
        sn = cosine_of(phase - 128)
        sh, sl = halves(sn)
        nh, nl = halves(-sn)
        mh[rows, 0:TOK] = ch
        ml[rows, 0:TOK] = cl
        mh[rows, TOK:] = sh
        ml[rows, TOK:] = sl
        mh[more, 0:TOK] = nh
        ml[more, 0:TOK] = nl
        mh[more, TOK:] = ch
        ml[more, TOK:] = cl

    @pl.loop(0, TOK // 64)
    def _(r):
        rows = pl.ds(pl.multiple_of(r * 64, 64), 64)
        more = pl.ds(pl.multiple_of(r * 64 + TOK, 64), 64)
        phase = krow[0:1, :] * (iota((64, KEPT), 0) + r * 64)
        ch, cl = halves(cosine_of(phase))
        sn = cosine_of(phase - 128)
        sh, sl = halves(sn)
        nh, nl = halves(-sn)
        th[rows, 0:KEPT] = ch
        tl[rows, 0:KEPT] = cl
        th[rows, KEPT:] = nh
        tl[rows, KEPT:] = nl
        th[more, 0:KEPT] = sh
        tl[more, 0:KEPT] = sl
        th[more, KEPT:] = ch
        tl[more, KEPT:] = cl

    @pl.loop(0, OUTER)
    def _(a):
        i, n = iota((128, 256), 0), iota((128, 256), 1)
        phase = ((i >> 5) * 8 + a) * ((n >> 5) & 3) + 8 * (n >> 7)
        hi, lo = halves(jnp.where((i & 31) == (n & 31), cosine_of(phase * 16), 0.0))
        dm[a, 0:128, :] = hi
        dm[a, 128:256, :] = lo
        n, i = iota((256, 128), 0), iota((256, 128), 1)
        phase = ((i >> 5) * 8 + a) * ((n >> 5) & 3) + 8 * (n >> 7)
        hi, lo = halves(jnp.where((i & 31) == (n & 31), cosine_of(phase * 16), 0.0))
        eh[a] = hi
        el[a] = lo

    @pl.loop(0, ROWS)
    def _(r):
        rows = pl.ds(pl.multiple_of(r * STEP, STEP), STEP)
        j = iota((STEP, 128), 0) + r * STEP
        alpha = (j * (iota((STEP, 128), 1) >> 5)).astype(F32) * (2 * math.pi / LENGTH)
        beta = (j * INNER).astype(F32) * (2 * math.pi / LENGTH)
        tw[0, rows, :] = sine(math.pi / 2 - alpha)
        tw[1, rows, :] = sine(alpha)
        tw[2, rows, :] = sine(math.pi / 2 - beta)
        tw[3, rows, :] = sine(beta)

    collect(xr, xs, xsend, xrecv)

    @pl.loop(0, OUTER)
    def _(a):
        for k, part in enumerate(swap([xr[OUTER * l + a] for l in range(INNER)], perm)):
            rq[QUARTER * k : QUARTER * (k + 1), 0:128] = part
            rq[QUARTER * k : QUARTER * (k + 1), 128:256] = part
        g[a] = dot(rq[...], dm[a])

    def twists(rows):
        tc, ts = tw[0, rows, :], tw[1, rows, :]
        uc, us = tw[2, rows, :], tw[3, rows, :]
        found = []
        for p in range(OUTER):
            found.append((tc, ts))
            if p + 1 < OUTER:
                tc, ts = tc * uc - ts * us, ts * uc + tc * us
        return found

    @pl.loop(0, ROWS)
    def _(r):
        rows = pl.ds(pl.multiple_of(r * STEP, STEP), STEP)
        more = pl.ds(pl.multiple_of(r * STEP + TOK, STEP), STEP)
        first = transform([(g[a, rows, 0:128], g[a, rows, 128:256]) for a in range(OUTER)], -1)
        for p, ((re, im), (tc, ts)) in enumerate(zip(first, twists(rows))):
            cols = slice(128 * (p % 2), 128 * (p % 2) + 128)
            fst[p // 2, rows, cols] = (re * tc + im * ts).astype(BF16)
            fst[p // 2, more, cols] = (im * tc - re * ts).astype(BF16)

    collect(fr, fs, fsend, frecv)

    @pl.loop(0, OUTER // 2)
    def _(w):
        for half in range(2):
            p = 2 * w + half
            cols = slice(128 * half, 128 * half + 128)
            for k, part in enumerate(swap([fr[INNER * p + l] for l in range(INNER)], perm)):
                fm[0, UNIT * k : UNIT * (k + 1), cols] = part[0:UNIT]
                fm[1, UNIT * k : UNIT * (k + 1), cols] = part[UNIT:]
        spectrum = dot(mh[...], fst[w]) + dot(ml[...], fst[w])
        sr, si = spectrum[0:KEPT], spectrum[KEPT:]
        f_re, f_im = fm[0].astype(F32), fm[1].astype(F32)
        product = jnp.concatenate([f_re * sr - f_im * si, f_re * si + f_im * sr], axis=0)
        hi, lo = halves(product)
        b[w] = dot(th[...], hi) + dot(tl[...], hi) + dot(th[...], lo)

    @pl.loop(0, ROWS)
    def _(r):
        rows = pl.ds(pl.multiple_of(r * STEP, STEP), STEP)
        more = pl.ds(pl.multiple_of(r * STEP + TOK, STEP), STEP)
        turned = []
        for p, (tc, ts) in enumerate(twists(rows)):
            cols = slice(128 * (p % 2), 128 * (p % 2) + 128)
            re, im = b[p // 2, rows, cols], b[p // 2, more, cols]
            turned.append(
                (
                    (re * tc - im * ts).astype(BF16).astype(F32),
                    (re * ts + im * tc).astype(BF16).astype(F32),
                )
            )
        for a, (re, im) in enumerate(transform(turned, 1)):
            hi, lo = halves(re)
            vh[a, rows, 0:128] = hi
            vl[a, rows, 0:128] = lo
            hi, lo = halves(im)
            vh[a, rows, 128:256] = hi
            vl[a, rows, 128:256] = lo

    @pl.loop(0, OUTER)
    def _(i):
        a = lax.rem(lax.rem(me, OUTER) + i, OUTER)
        c = dot(vh[a], eh[a]) + dot(vl[a], eh[a]) + dot(vh[a], el[a])
        c = (c * (1.0 / LENGTH)).astype(BF16)
        for l, part in enumerate(swap([c[QUARTER * k : QUARTER * (k + 1)] for k in range(INNER)], perm)):
            deliver(OUTER * l + a, part, cs, cr, csend, crecv)

    collect(cr, cs, csend, crecv)

    @pl.loop(0, OUTER)
    def _(tile):
        for k, part in enumerate(swap([cr[INNER * tile + q] for q in range(INNER)], perm)):
            rows = slice(QUARTER * k, QUARTER * (k + 1))
            direct = skip[0:1, lanes(tile)] * kv[rows, lanes(tile)].astype(F32)
            hid[rows, lanes(tile)] = (
                gate[rows, lanes(tile)].astype(F32) * (part.astype(F32) + direct)
            ).astype(BF16)

    def cols(t):
        return pl.ds(pl.multiple_of(t * WIDTH, WIDTH), WIDTH)

    if tensor:
        top, bottom = slice(0, TOK // 2), slice(TOK // 2, TOK)

        def gather(index, src, rows, block, to):
            return remote(
                src, out.at[rows, cols(block)], gsend.at[index], grecv.at[index], to, "tensor"
            )

        every = slice(0, TOK)
        sends = [
            gather(0, hid, every, ten, zp),
            gather(1, hid, every, ten, yp),
            gather(2, hid, every, ten, ym),
        ]
        for c in sends:
            c.start()
        keep = pltpu.make_async_copy(hid, out.at[:, cols(ten)], local)
        keep.start()

        def arrived(index, rows, block):
            gather(index, out.at[rows, cols(block)], rows, block, zp).wait_recv()

        def relay(index, rows, block, to):
            c = gather(index, out.at[rows, cols(block)], rows, block, to)
            c.start()
            sends.append(c)

        arrived(0, every, zp)
        relay(3, every, zp, yp)
        relay(4, every, zp, ym)
        arrived(1, every, ym)
        relay(5, top, ym, yp)
        arrived(2, every, yp)
        relay(6, bottom, yp, ym)
        arrived(3, every, far + down)
        relay(7, top, far + down, yp)
        arrived(4, every, far + up)
        relay(8, bottom, far + up, ym)
        across = lax.rem(y + 2, 4)
        arrived(5, top, zl * 4 + across)
        arrived(6, bottom, zl * 4 + across)
        arrived(7, top, far + across)
        arrived(8, bottom, far + across)
        for c in sends:
            c.wait_send()
        keep.wait()
    else:
        pltpu.sync_copy(hid, out)

    settle(xr, xs, xsend, xrecv)
    settle(fr, fs, fsend, frecv)
    settle(cr, cs, csend, crecv)


def gathered_hidden(keyval, gating, skip_gain, filter_values, blocks, tensor):
    me = lax.axis_index("seq")
    groups = blocks.shape[0]
    group = me * groups // SEQ
    match = group == jnp.arange(groups, dtype=jnp.int32)
    kept = jnp.sum(jnp.where(match[:, None], blocks, 0), axis=0)
    kept = (kept[:, None] * 2 + jnp.arange(2, dtype=jnp.int32)[None, :]).reshape(KEPT)
    kcol = jnp.broadcast_to(kept[:, None], (KEPT, 128))
    krow = jnp.broadcast_to(kept[None, :], (8, KEPT))
    vmem = pl.BlockSpec(memory_space=pltpu.VMEM)
    dma = pltpu.SemaphoreType.DMA

    def buf(*shape, dtype=BF16):
        return pltpu.VMEM(shape, dtype)

    wide = WIDTH * (8 if tensor else 1)
    return pl.pallas_call(
        functools.partial(kernel, tensor),
        out_shape=jax.ShapeDtypeStruct((TOK, wide), BF16),
        in_specs=[vmem] * 6,
        out_specs=pl.BlockSpec(memory_space=pl.ANY),
        scratch_shapes=[
            buf(SEQ, 128, 128), buf(SEQ, 128, 128),
            buf(SEQ, 64, 128), buf(SEQ, 64, 128),
            buf(256, 1024), buf(256, 1024), buf(1024, 256), buf(1024, 256),
            buf(8, 256, 256), buf(8, 256, 128), buf(8, 256, 128), buf(512, 512),
            buf(4, 512, 128, dtype=F32), buf(512, 256), buf(8, 512, 256, dtype=F32),
            buf(4, 1024, 256), buf(2, 128, 256), buf(4, 1024, 256, dtype=F32),
            buf(8, 512, 256), buf(8, 512, 256),
            buf(SEQ, 128, 128), buf(SEQ, 128, 128), buf(TOK, WIDTH),
            dma((SEQ,)), dma((SEQ,)), dma((SEQ,)), dma((SEQ,)), dma((SEQ,)), dma((SEQ,)),
            dma((9,)), dma((9,)), dma,
        ],
        compiler_params=pltpu.CompilerParams(
            collective_id=0, has_side_effects=True, vmem_limit_bytes=50 * 2**20
        ),
        cost_estimate=pl.CostEstimate(flops=10**11, bytes_accessed=10**8, transcendentals=0),
    )(keyval, gating, skip_gain.reshape(1, WIDTH), filter_values.reshape(2048, 128), kcol, krow)


def body(keyval, gating, skip_gain, filter_values, blocks, out_weight):
    whole_weight = lax.all_gather(out_weight, "seq", axis=0, tiled=True)
    full_hidden = gathered_hidden(keyval, gating, skip_gain, filter_values, blocks, True)
    mixed = jnp.dot(full_hidden, whole_weight, preferred_element_type=F32)
    return mixed.astype(BF16)


def solution(mesh):
    placed = (
        P("seq", "tensor"),
        P("seq", "tensor"),
        P("tensor"),
        P(None, None, None, "seq", "tensor"),
        P("tensor", None),
        P("seq", "tensor"),
    )
    return jax.shard_map(
        body, mesh=mesh, in_specs=placed, out_specs=P("seq", "tensor"), check_vma=False
    )
```

time: 410 us -> 272 us (0.66)
  waiting for transfers between devices: 279 us -> 0.73 us
  Pallas kernels: 0 us -> 234 us
  matrix products: 47.4 us -> 15.6 us
  local copies, waits for them, and re-layouts: 27.1 us -> 4.58 us
  starting transfers between devices: 19.8 us -> 0.01 us
  other arithmetic: 19.3 us -> 0.86 us
    pallas_call x0 -> x1, Pallas kernels: none -> 234 us  [gathered_hidden(): pl.pallas_call(functools.partial(kernel, tensor), out_shape=jax.ShapeDtyp...]
    all_gather x1, waiting for transfers between devices: 122 us -> 0.02 us  [body(): whole_weight = lax.all_gather(out_weight, 'seq', axis=0, tiled=True)]
    all_gather x1 -> x0, waiting for transfers between devices: 88.6 us -> none  [body(): full_hidden = lax.all_gather(hidden, 'tensor', axis=1, tiled=True)]
    all_to_all x3 -> x0, waiting for transfers between devices: 67.2 us -> none  [the longest x1 29.2 us: body(): lax.all_to_all(done, 'seq', split_axis=0, concat_axis=1, tiled=True)]
    dot_general x13 -> x1, matrix products: 47.4 us -> 15.6 us  [body(): mixed = jnp.dot(full_hidden, whole_weight, preferred_element_type=F32)]
    all_to_all x3 -> x0, starting transfers between devices: 19.7 us -> none  [the longest x1 10.9 us: body(): lax.all_to_all(keyval, 'seq', split_axis=1, concat_axis=0, tiled=True)]
    all_to_all x1 -> x0, other arithmetic: 16.2 us -> none  [body(): lax.all_to_all(filter_values, 'seq', split_axis=4, concat_axis=3, tiled=T...]
    squeeze x4 -> x0, local copies, waits for them, and re-layouts: 8.11 us -> none  [the longest x2 4.1 us: whole_conv(): filter_group[1].reshape(-1, cycle_size, unit).transpose(1, 0, 2)]
  transfers between devices with their start and end apart: 5 -> 1, of which waited for: 5 -> 0; matrix products, arithmetic and copies ran while one was open for 5% -> 0% of each run, Pallas kernels for 0% -> 87%
where the time goes in v1:
time: 272 us; the launch traced here: 269 us
  Pallas kernels  234 us (86%)
  matrix products  15.6 us (6%)
  between operations  13.5 us (5%)
  local copies, waits for them, and re-layouts  4.58 us (2%)
    pallas_call x1, Pallas kernels, gathered_hidden(): pl.pallas_call(functools.partial(kernel, tensor), out_shape=jax.ShapeDtyp...  234 us
    dot_general x1, matrix products, body(): mixed = jnp.dot(full_hidden, whole_weight, preferred_element_type=F32)  15.6 us
  transfers between devices with their start and end apart: 1, of which 0 were waited for; matrix products, arithmetic and copies ran while one was open for 0% of the time, Pallas kernels for 87%

profile of v1, /device:TPU:33, one launch (start us, length us, event | category | flops | bytes accessed | tf_op | source)
XLA Modules:
  0.0 269.3 jit_solution(7825329190424326598)
XLA Ops:
  6.5 0.0 all-gather.2.cloned.1.call-start
  6.5 0.7 all-gather.2.cloned.1.call-update
  7.3 0.8 select_reduce_fusion
  8.1 0.1 iota_add_fusion
  8.1 0.1 add.28
  8.3 0.1 broadcast_in_dim.27.kcol
  8.4 0.0 copy-start
  8.4 1.2 copy-done
  9.6 0.0 copy-start.1
  9.6 1.2 copy-done.1
  10.8 0.0 copy-start.2
  10.8 1.2 copy-done.2
  12.1 0.0 copy-start.3
  12.1 0.7 copy-done.3
  12.7 234.1 %shard_map.64 = bf16[512,8192]{1,0:T(8,128)(2,1)} custom-call(bf16[512,1024]{1,0:T(8,128)(2,1)S(1)} %copy-done, bf16[512,1024]{1,0:T(8,128)(2,1)S(1)} %copy-done.1, f32[1,1024]{1,0:T(1,128)S(1)} %bitcast.5, f32[2048,128]{1,0:T(8,128)S(1)} %bitcast.4, s32[128,128]{1,0:T(8,128)S(1)} %broadcast_in_dim.27.kcol, s32[8,128]{1,0:T(8,128)S(1)} %broadcast_in_dim.28.krow), custom_call_target="tpu_custom_call" | custom-call | flops 99999997952 | bytes 100000000 | tf_op jit(solution)/shard_map/pallas_call | solution.py:395
  246.9 0.0 all-gather.2.cloned.1.call-done
  246.9 15.6 %convolution_convert_fusion = bf16[512,1024]{1,0:T(8,128)(2,1)} fusion(bf16[512,8192]{1,0:T(8,128)(2,1)} %shard_map.64, bf16[8192,1024]{1,0:T(8,128)(2,1)} %all-gather.2.cloned.1.call-done), kind=kOutput, calls=%fused_computation | convolution fusion | flops 8590458880 | bytes 26214400 | tf_op jit(solution)/shard_map/dot_general | solution.py:422
  (3 shorter events, 0.0 us)
Async XLA Ops:
  6.5 240.4 %all-gather.2.cloned.1.call-start = ((), (), s32[]{:S(2)}) async-start(), calls=%async_computation | async-start | bytes 17301504 | tf_op jit(solution)/shard_map/all_gather | solution.py:420
  8.4 1.2 copy-start
  9.6 1.2 copy-start.1
  10.8 1.2 copy-start.2
  12.1 0.7 copy-start.3
Sparse Core Ops, SparseCore 0:
  9.9 187.3 all-gather.1

commit v2 on v1

--- a/solution.py
+++ b/solution.py
@@ -1,4 +1,3 @@
-import functools
 import math
 
 import jax
@@ -19,6 +18,7 @@
 KEPT = 128
 STEP = 16
 ROWS = TOK // STEP
+SPLIT = 288
 LENGTH = SEQ * TOK
 F32 = jnp.float32
 BF16 = jnp.bfloat16
@@ -87,17 +87,31 @@
 
 
 def kernel(
-    tensor, kv, gate, skip, filt, kcol, krow, out,
-    xs, xr, fs, fr, mh, ml, th, tl, dm, eh, el, perm, tw, rq, g, fst, fm, b, vh, vl, cs, cr, hid,
-    xsend, xrecv, fsend, frecv, csend, crecv, gsend, grecv, local,
+    kv_in, gate_in, skip, filt_in, kcol, krow, weight_in, out,
+    kv, gate, filt, xs, xr, fs, fr, mh, ml, th, tl, dm, eh, el, perm, tw, rq, g, fst, fm, vh, vl,
+    cs, cr, gath, wv, acc,
+    xsend, xrecv, fsend, frecv, csend, crecv, gsend, grecv, wsend, wrecv, local,
 ):
     me = lax.axis_index("seq")
     ten = lax.axis_index("tensor")
     zl, y = ten // 4, lax.rem(ten, 4)
-    far = (1 - zl) * 4
+    far, near = (1 - zl) * 4, zl * 4
     zp = far + y
-    up, down = lax.rem(y + 1, 4), lax.rem(y + 3, 4)
-    yp, ym = zl * 4 + up, zl * 4 + down
+    up, down, across = lax.rem(y + 1, 4), lax.rem(y + 3, 4), lax.rem(y + 2, 4)
+    yp, ym = near + up, near + down
+    core = lax.rem(me, 2)
+    zh = lax.rem(me // 2, 4)
+    x = me // 8
+    first_core = core == 0
+
+    loads = [
+        pltpu.make_async_copy(kv_in, kv, local.at[0]),
+        pltpu.make_async_copy(weight_in, wv.at[me], local.at[1]),
+        pltpu.make_async_copy(filt_in, filt, local.at[2]),
+        pltpu.make_async_copy(gate_in, gate, local.at[3]),
+    ]
+    for c in loads:
+        c.start()
 
     barrier = pltpu.get_barrier_semaphore()
 
@@ -107,9 +121,8 @@
             barrier, inc=1, device_id={"seq": lax.rem(me + i, SEQ)}, device_id_type=MESH
         )
 
-    if tensor:
-        for t in (zp, yp, ym):
-            pl.semaphore_signal(barrier, inc=1, device_id={"tensor": t}, device_id_type=MESH)
+    for t in (zp, yp, ym):
+        pl.semaphore_signal(barrier, inc=1, device_id={"tensor": t}, device_id_type=MESH)
 
     @pl.loop(0, 8)
     def _(r):
@@ -150,7 +163,35 @@
             src = lax.rem(me + i, SEQ)
             remote(staged.at[src], landed.at[src], ss.at[src], rs.at[src], src).wait_send()
 
-    pl.semaphore_wait(barrier, SEQ - 1 + (3 if tensor else 0))
+    def node(dx, dz, other=False):
+        c = 1 - core if other else core
+        return lax.rem(x + dx, 4) * 8 + lax.rem(zh + dz, 4) * 2 + c
+
+    sent = []
+
+    def push(block, dev):
+        index = len(sent)
+        c = remote(wv.at[block], wv.at[block], wsend.at[index], wrecv.at[block], dev)
+        sent.append(c)
+        return c
+
+    def pushed(block):
+        remote(wv.at[block], wv.at[block], wsend.at[0], wrecv.at[block], node(0, 0, True)).wait_recv()
+
+    def spread(dz):
+        block = node(0, dz)
+        for dev in (node(1, 0), node(3, 0), node(0, 0, True)):
+            push(block, dev).start()
+
+    def onward(dz):
+        for dx in (3, 1):
+            pushed(node(dx, dz))
+            push(node(dx, dz), node(0, 0, True)).start()
+        block = jnp.where(first_core, node(3, dz), node(1, dz))
+        push(block, jnp.where(first_core, node(1, 0), node(3, 0))).start()
+
+    loads[0].wait()
+    pl.semaphore_wait(barrier, SEQ - 1 + 3)
 
     @pl.loop(0, OUTER)
     def _(i):
@@ -158,6 +199,8 @@
         parts = [kv[QUARTER * k : QUARTER * (k + 1), lanes(tile)] for k in range(INNER)]
         for q, part in enumerate(swap(parts, perm)):
             deliver(tile * INNER + q, part, xs, xr, xsend, xrecv)
+
+    loads[2].wait()
 
     @pl.loop(0, OUTER)
     def _(i):
@@ -171,6 +214,9 @@
             parts.append(jnp.concatenate(pair, axis=0))
         for q, part in enumerate(swap(parts, perm)):
             deliver(tile * INNER + q, part, fs, fr, fsend, frecv)
+
+    loads[1].wait()
+    spread(0)
 
     @pl.loop(0, KEPT // STEP)
     def _(r):
@@ -233,6 +279,8 @@
         tw[3, rows, :] = sine(beta)
 
     collect(xr, xs, xsend, xrecv)
+    for dz in (1, 3):
+        push(me, node(0, dz)).start()
 
     @pl.loop(0, OUTER)
     def _(a):
@@ -276,16 +324,17 @@
         f_re, f_im = fm[0].astype(F32), fm[1].astype(F32)
         product = jnp.concatenate([f_re * sr - f_im * si, f_re * si + f_im * sr], axis=0)
         hi, lo = halves(product)
-        b[w] = dot(th[...], hi) + dot(tl[...], hi) + dot(th[...], lo)
+        for part in range(2):
+            rows = slice(TOK * part, TOK * (part + 1))
+            g[2 * w + part] = dot(th[rows], hi) + dot(tl[rows], hi) + dot(th[rows], lo)
 
     @pl.loop(0, ROWS)
     def _(r):
         rows = pl.ds(pl.multiple_of(r * STEP, STEP), STEP)
-        more = pl.ds(pl.multiple_of(r * STEP + TOK, STEP), STEP)
         turned = []
         for p, (tc, ts) in enumerate(twists(rows)):
             cols = slice(128 * (p % 2), 128 * (p % 2) + 128)
-            re, im = b[p // 2, rows, cols], b[p // 2, more, cols]
+            re, im = g[p // 2 * 2, rows, cols], g[p // 2 * 2 + 1, rows, cols]
             turned.append(
                 (
                     (re * tc - im * ts).astype(BF16).astype(F32),
@@ -308,7 +357,19 @@
         for l, part in enumerate(swap([c[QUARTER * k : QUARTER * (k + 1)] for k in range(INNER)], perm)):
             deliver(OUTER * l + a, part, cs, cr, csend, crecv)
 
+    for dz in (3, 1):
+        pushed(node(0, dz))
+    push(
+        jnp.where(first_core, node(0, 3), node(0, 1)),
+        jnp.where(first_core, node(0, 1), node(0, 3)),
+    ).start()
+    spread(1)
+    spread(3)
+    onward(0)
+    loads[3].wait()
+
     collect(cr, cs, csend, crecv)
+    hid = gath.at[ten]
 
     @pl.loop(0, OUTER)
     def _(tile):
@@ -319,108 +380,122 @@
                 gate[rows, lanes(tile)].astype(F32) * (part.astype(F32) + direct)
             ).astype(BF16)
 
-    def cols(t):
-        return pl.ds(pl.multiple_of(t * WIDTH, WIDTH), WIDTH)
-
-    if tensor:
-        top, bottom = slice(0, TOK // 2), slice(TOK // 2, TOK)
-
-        def gather(index, src, rows, block, to):
-            return remote(
-                src, out.at[rows, cols(block)], gsend.at[index], grecv.at[index], to, "tensor"
-            )
-
-        every = slice(0, TOK)
-        sends = [
-            gather(0, hid, every, ten, zp),
-            gather(1, hid, every, ten, yp),
-            gather(2, hid, every, ten, ym),
-        ]
-        for c in sends:
-            c.start()
-        keep = pltpu.make_async_copy(hid, out.at[:, cols(ten)], local)
-        keep.start()
-
-        def arrived(index, rows, block):
-            gather(index, out.at[rows, cols(block)], rows, block, zp).wait_recv()
-
-        def relay(index, rows, block, to):
-            c = gather(index, out.at[rows, cols(block)], rows, block, to)
-            c.start()
-            sends.append(c)
-
-        arrived(0, every, zp)
-        relay(3, every, zp, yp)
-        relay(4, every, zp, ym)
-        arrived(1, every, ym)
-        relay(5, top, ym, yp)
-        arrived(2, every, yp)
-        relay(6, bottom, yp, ym)
-        arrived(3, every, far + down)
-        relay(7, top, far + down, yp)
-        arrived(4, every, far + up)
-        relay(8, bottom, far + up, ym)
-        across = lax.rem(y + 2, 4)
-        arrived(5, top, zl * 4 + across)
-        arrived(6, bottom, zl * 4 + across)
-        arrived(7, top, far + across)
-        arrived(8, bottom, far + across)
-        for c in sends:
-            c.wait_send()
-        keep.wait()
-    else:
-        pltpu.sync_copy(hid, out)
-
+    every, upper, lower = slice(0, TOK), slice(0, SPLIT), slice(SPLIT, TOK)
+    gathers = []
+
+    def gather(block, rows, to, side=0):
+        c = remote(
+            gath.at[block, rows], gath.at[block, rows],
+            gsend.at[len(gathers)], grecv.at[side, block], to, "tensor",
+        )
+        gathers.append(c)
+        c.start()
+
+    def arrived(block, rows, side=0):
+        remote(
+            gath.at[block, rows], gath.at[block, rows],
+            gsend.at[0], grecv.at[side, block], zp, "tensor",
+        ).wait_recv()
+
+    gather(ten, every, yp)
+    gather(ten, every, ym)
+    gather(ten, every, zp)
+    pushed(node(0, 2))
+    spread(2)
+    arrived(zp, every)
+    gather(zp, upper, yp)
+    gather(zp, upper, ym)
+    ahead = jnp.where(first_core, yp, ym)
+    arrived(ym, every)
+    arrived(yp, every)
+    gather(jnp.where(first_core, ym, yp), every, ahead)
+    gather(ym, lower, zp, 1)
+    gather(yp, lower, zp, 1)
+    onward(1)
+    onward(3)
+    onward(2)
+    arrived(far + down, upper)
+    arrived(far + up, upper)
+    gather(jnp.where(first_core, far + down, far + up), upper, ahead)
+    arrived(near + across, every)
+    gather(near + across, lower, zp, 1)
+    for dz in range(4):
+        pushed(node(2, dz))
+        push(node(2, dz), node(0, 0, True)).start()
+    for dx in range(4):
+        for dz in range(4):
+            pushed(node(dx, dz, True))
+
+    def project(block, start=False):
+        @pl.loop(0, 4)
+        def _(n):
+            cols = pl.ds(pl.multiple_of(n * 256, 256), 256)
+            w = wv[pl.ds(INNER * block, INNER), :, cols].reshape(WIDTH, 256)
+            part = dot(gath[block], w)
+            acc[:, cols] = part if start else acc[:, cols] + part
+
+    project(ten, True)
+    project(zp)
+    project(ym)
+    project(yp)
+    project(near + across)
+    for block in (far + down, far + up):
+        arrived(block, lower, 1)
+        project(block)
+    arrived(far + across, upper)
+    arrived(far + across, lower, 1)
+    project(far + across)
+    out[...] = acc[...].astype(BF16)
+    for c in gathers:
+        c.wait_send()
+    for c in sent:
+        c.wait_send()
     settle(xr, xs, xsend, xrecv)
     settle(fr, fs, fsend, frecv)
     settle(cr, cs, csend, crecv)
 
 
-def gathered_hidden(keyval, gating, skip_gain, filter_values, blocks, tensor):
+def body(keyval, gating, skip_gain, filter_values, blocks, out_weight):
     me = lax.axis_index("seq")
     groups = blocks.shape[0]
-    group = me * groups // SEQ
-    match = group == jnp.arange(groups, dtype=jnp.int32)
+    match = me * groups // SEQ == jnp.arange(groups, dtype=jnp.int32)
     kept = jnp.sum(jnp.where(match[:, None], blocks, 0), axis=0)
     kept = (kept[:, None] * 2 + jnp.arange(2, dtype=jnp.int32)[None, :]).reshape(KEPT)
     kcol = jnp.broadcast_to(kept[:, None], (KEPT, 128))
     krow = jnp.broadcast_to(kept[None, :], (8, KEPT))
     vmem = pl.BlockSpec(memory_space=pltpu.VMEM)
+    away = pl.BlockSpec(memory_space=pl.ANY)
     dma = pltpu.SemaphoreType.DMA
 
     def buf(*shape, dtype=BF16):
         return pltpu.VMEM(shape, dtype)
 
-    wide = WIDTH * (8 if tensor else 1)
     return pl.pallas_call(
-        functools.partial(kernel, tensor),
-        out_shape=jax.ShapeDtypeStruct((TOK, wide), BF16),
-        in_specs=[vmem] * 6,
-        out_specs=pl.BlockSpec(memory_space=pl.ANY),
+        kernel,
+        out_shape=jax.ShapeDtypeStruct((TOK, WIDTH), BF16),
+        in_specs=[away, away, vmem, away, vmem, vmem, away],
+        out_specs=vmem,
         scratch_shapes=[
+            buf(TOK, WIDTH), buf(TOK, WIDTH), buf(2048, 128, dtype=F32),
             buf(SEQ, 128, 128), buf(SEQ, 128, 128),
             buf(SEQ, 64, 128), buf(SEQ, 64, 128),
             buf(256, 1024), buf(256, 1024), buf(1024, 256), buf(1024, 256),
             buf(8, 256, 256), buf(8, 256, 128), buf(8, 256, 128), buf(512, 512),
             buf(4, 512, 128, dtype=F32), buf(512, 256), buf(8, 512, 256, dtype=F32),
-            buf(4, 1024, 256), buf(2, 128, 256), buf(4, 1024, 256, dtype=F32),
+            buf(4, 1024, 256), buf(2, 128, 256),
             buf(8, 512, 256), buf(8, 512, 256),
-            buf(SEQ, 128, 128), buf(SEQ, 128, 128), buf(TOK, WIDTH),
+            buf(SEQ, 128, 128), buf(SEQ, 128, 128), buf(8, TOK, WIDTH),
+            buf(SEQ, 256, WIDTH), buf(TOK, WIDTH, dtype=F32),
             dma((SEQ,)), dma((SEQ,)), dma((SEQ,)), dma((SEQ,)), dma((SEQ,)), dma((SEQ,)),
-            dma((9,)), dma((9,)), dma,
+            dma((10,)), dma((2, 8)), dma((31,)), dma((SEQ,)), dma((4,)),
         ],
         compiler_params=pltpu.CompilerParams(
-            collective_id=0, has_side_effects=True, vmem_limit_bytes=50 * 2**20
+            collective_id=0, has_side_effects=True, vmem_limit_bytes=60 * 2**20
         ),
-        cost_estimate=pl.CostEstimate(flops=10**11, bytes_accessed=10**8, transcendentals=0),
-    )(keyval, gating, skip_gain.reshape(1, WIDTH), filter_values.reshape(2048, 128), kcol, krow)
-
-
-def body(keyval, gating, skip_gain, filter_values, blocks, out_weight):
-    whole_weight = lax.all_gather(out_weight, "seq", axis=0, tiled=True)
-    full_hidden = gathered_hidden(keyval, gating, skip_gain, filter_values, blocks, True)
-    mixed = jnp.dot(full_hidden, whole_weight, preferred_element_type=F32)
-    return mixed.astype(BF16)
+    )(
+        keyval, gating, skip_gain.reshape(1, WIDTH), filter_values.reshape(2048, 128),
+        kcol, krow, out_weight,
+    )
 
 
 def solution(mesh):

time: 272 us -> 181 us (0.67)
  Pallas kernels: 234 us -> 176 us
  matrix products: 15.6 us -> 0 us
  between operations: 13.5 us -> 0.02 us
    pallas_call x1, Pallas kernels: 234 us -> 176 us  [body(): pl.pallas_call(kernel, out_shape=jax.ShapeDtypeStruct((TOK, WIDTH), BF16)...]
    dot_general x1 -> x0, matrix products: 15.6 us -> none  [body(): mixed = jnp.dot(full_hidden, whole_weight, preferred_element_type=F32)]
  transfers between devices with their start and end apart: 1 -> 0, of which waited for: 0 -> 0; matrix products, arithmetic and copies ran while one was open for 0% -> 0% of each run, Pallas kernels for 87% -> 0%
where the time goes in v2:
time: 181 us; the launch traced here: 180 us
  Pallas kernels  176 us (97%)
  local copies, waits for them, and re-layouts  4.39 us (2%)
    pallas_call x1, Pallas kernels, body(): pl.pallas_call(kernel, out_shape=jax.ShapeDtypeStruct((TOK, WIDTH), BF16)...  176 us

profile of v2, /device:TPU:33, one launch (start us, length us, event | category | flops | bytes accessed | tf_op | source)
XLA Modules:
  0.0 180.4 jit_solution(2323433514510657588)
XLA Ops:
  0.0 0.0 copy-start
  0.0 0.7 copy-done
  0.7 0.1 select_reduce_fusion
  0.8 0.1 iota_add_fusion
  0.9 0.1 add.28
  1.0 0.6 broadcast_in_dim.28.krow
  1.6 0.7 broadcast_in_dim.27.kcol
  2.3 175.9 %shard_map.64 = bf16[512,1024]{1,0:T(8,128)(2,1)} custom-call(bf16[512,1024]{1,0:T(8,128)(2,1)} %kv_in.1, bf16[512,1024]{1,0:T(8,128)(2,1)} %gate_in.1, f32[1,1024]{1,0:T(1,128)} %bitcast.3, f32[2048,128]{1,0:T(8,128)} %bitcast.2, s32[128,128]{1,0:T(8,128)} %broadcast_in_dim.27.kcol, s32[8,128]{1,0:T(8,128)} %broadcast_in_dim.28.krow, ...), custom_call_target="tpu_custom_call" | custom-call | tf_op jit(solution)/shard_map/pallas_call | solution.py:473
  178.2 2.3 %copy.8 = bf16[512,1024]{1,0:T(8,128)(2,1)} copy(bf16[512,1024]{1,0:T(8,128)(2,1)} %shard_map.64) | data formatting | bytes 2097152
  (2 shorter events, 0.0 us)
Async XLA Ops:
  0.0 0.7 copy-start

commit v3 on v2

--- a/solution.py
+++ b/solution.py
@@ -18,7 +18,7 @@
 KEPT = 128
 STEP = 16
 ROWS = TOK // STEP
-SPLIT = 288
+HALF = TOK // 2
 LENGTH = SEQ * TOK
 F32 = jnp.float32
 BF16 = jnp.bfloat16
@@ -87,8 +87,8 @@
 
 
 def kernel(
-    kv_in, gate_in, skip, filt_in, kcol, krow, weight_in, out,
-    kv, gate, filt, xs, xr, fs, fr, mh, ml, th, tl, dm, eh, el, perm, tw, rq, g, fst, fm, vh, vl,
+    kv_in, gate_in, skip, filt_in, blocks, weight_in, out,
+    kcol, krow, kv, gate, filt, xs, xr, fs, fr, mh, ml, th, tl, dm, eh, el, perm, tw, rq, g, fst, fm, vh, vl,
     cs, cr, gath, wv, acc,
     xsend, xrecv, fsend, frecv, csend, crecv, gsend, grecv, wsend, wrecv, local,
 ):
@@ -217,6 +217,19 @@
 
     loads[1].wait()
     spread(0)
+
+    group = iota((OUTER, 64), 0) == me // INNER
+    listed = jnp.sum(jnp.where(group, blocks[...].astype(F32), 0.0), axis=0, keepdims=True)
+    own = iota((KEPT, 64), 1) == (iota((KEPT, 64), 0) >> 1)
+    column = jnp.sum(jnp.where(own, listed, 0.0), axis=1, keepdims=True)
+    column = column.astype(jnp.int32) * 2 + (iota((KEPT, 1), 0) & 1)
+    kcol[...] = jnp.broadcast_to(column, (KEPT, 128))
+    own = iota((64, 64), 1) == iota((64, 64), 0)
+    upright = jnp.sum(jnp.where(own, listed, 0.0), axis=1, keepdims=True)
+    own = iota((64, KEPT), 0) == (iota((64, KEPT), 1) >> 1)
+    row = jnp.sum(jnp.where(own, upright, 0.0), axis=0, keepdims=True)
+    row = row.astype(jnp.int32) * 2 + (iota((1, KEPT), 1) & 1)
+    krow[...] = jnp.broadcast_to(row, (8, KEPT))
 
     @pl.loop(0, KEPT // STEP)
     def _(r):
@@ -328,34 +341,41 @@
             rows = slice(TOK * part, TOK * (part + 1))
             g[2 * w + part] = dot(th[rows], hi) + dot(tl[rows], hi) + dot(th[rows], lo)
 
-    @pl.loop(0, ROWS)
-    def _(r):
-        rows = pl.ds(pl.multiple_of(r * STEP, STEP), STEP)
-        turned = []
-        for p, (tc, ts) in enumerate(twists(rows)):
-            cols = slice(128 * (p % 2), 128 * (p % 2) + 128)
-            re, im = g[p // 2 * 2, rows, cols], g[p // 2 * 2 + 1, rows, cols]
-            turned.append(
-                (
-                    (re * tc - im * ts).astype(BF16).astype(F32),
-                    (re * ts + im * tc).astype(BF16).astype(F32),
+    for half in range(2):
+
+        @pl.loop(half * (ROWS // 2), (half + 1) * (ROWS // 2))
+        def _(r):
+            rows = pl.ds(pl.multiple_of(r * STEP, STEP), STEP)
+            turned = []
+            for p, (tc, ts) in enumerate(twists(rows)):
+                cols = slice(128 * (p % 2), 128 * (p % 2) + 128)
+                re, im = g[p // 2 * 2, rows, cols], g[p // 2 * 2 + 1, rows, cols]
+                turned.append(
+                    (
+                        (re * tc - im * ts).astype(BF16).astype(F32),
+                        (re * ts + im * tc).astype(BF16).astype(F32),
+                    )
                 )
-            )
-        for a, (re, im) in enumerate(transform(turned, 1)):
-            hi, lo = halves(re)
-            vh[a, rows, 0:128] = hi
-            vl[a, rows, 0:128] = lo
-            hi, lo = halves(im)
-            vh[a, rows, 128:256] = hi
-            vl[a, rows, 128:256] = lo
-
-    @pl.loop(0, OUTER)
-    def _(i):
-        a = lax.rem(lax.rem(me, OUTER) + i, OUTER)
-        c = dot(vh[a], eh[a]) + dot(vl[a], eh[a]) + dot(vh[a], el[a])
-        c = (c * (1.0 / LENGTH)).astype(BF16)
-        for l, part in enumerate(swap([c[QUARTER * k : QUARTER * (k + 1)] for k in range(INNER)], perm)):
-            deliver(OUTER * l + a, part, cs, cr, csend, crecv)
+            for a, (re, im) in enumerate(transform(turned, 1)):
+                hi, lo = halves(re)
+                vh[a, rows, 0:128] = hi
+                vl[a, rows, 0:128] = lo
+                hi, lo = halves(im)
+                vh[a, rows, 128:256] = hi
+                vl[a, rows, 128:256] = lo
+
+        @pl.loop(0, OUTER)
+        def _(i):
+            a = lax.rem(lax.rem(me, OUTER) + i, OUTER)
+            rows = slice(HALF * half, HALF * (half + 1))
+            v, rest = vh[a, rows], vl[a, rows]
+            c = dot(v, eh[a]) + dot(rest, eh[a]) + dot(v, el[a])
+            c = (c * (1.0 / LENGTH)).astype(BF16)
+            parts = [c[64 * k : 64 * (k + 1)] for k in range(INNER)]
+            for l, part in enumerate(swap(parts, perm)):
+                deliver(
+                    OUTER * l + a, part, cs.at[half], cr.at[half], csend.at[half], crecv.at[half]
+                )
 
     for dz in (3, 1):
         pushed(node(0, dz))
@@ -368,60 +388,72 @@
     onward(0)
     loads[3].wait()
 
-    collect(cr, cs, csend, crecv)
     hid = gath.at[ten]
-
-    @pl.loop(0, OUTER)
-    def _(tile):
-        for k, part in enumerate(swap([cr[INNER * tile + q] for q in range(INNER)], perm)):
-            rows = slice(QUARTER * k, QUARTER * (k + 1))
-            direct = skip[0:1, lanes(tile)] * kv[rows, lanes(tile)].astype(F32)
-            hid[rows, lanes(tile)] = (
-                gate[rows, lanes(tile)].astype(F32) * (part.astype(F32) + direct)
-            ).astype(BF16)
-
-    every, upper, lower = slice(0, TOK), slice(0, SPLIT), slice(SPLIT, TOK)
     gathers = []
-
-    def gather(block, rows, to, side=0):
+    whole = [slice(HALF * half, HALF * (half + 1)) for half in range(2)]
+    ahead = jnp.where(first_core, yp, ym)
+
+    def gather(half, block, to):
         c = remote(
-            gath.at[block, rows], gath.at[block, rows],
-            gsend.at[len(gathers)], grecv.at[side, block], to, "tensor",
+            gath.at[block, whole[half]], gath.at[block, whole[half]],
+            gsend.at[len(gathers)], grecv.at[half, block], to, "tensor",
         )
         gathers.append(c)
         c.start()
 
-    def arrived(block, rows, side=0):
+    def arrived(half, block):
         remote(
-            gath.at[block, rows], gath.at[block, rows],
-            gsend.at[0], grecv.at[side, block], zp, "tensor",
+            gath.at[block, whole[half]], gath.at[block, whole[half]],
+            gsend.at[0], grecv.at[half, block], zp, "tensor",
         ).wait_recv()
 
-    gather(ten, every, yp)
-    gather(ten, every, ym)
-    gather(ten, every, zp)
+    def settled(half):
+        collect(cr.at[half], cs.at[half], csend.at[half], crecv.at[half])
+
+        @pl.loop(0, OUTER)
+        def _(tile):
+            parts = [cr[half, INNER * tile + q] for q in range(INNER)]
+            for k, part in enumerate(swap(parts, perm)):
+                rows = slice(HALF * half + 64 * k, HALF * half + 64 * (k + 1))
+                direct = skip[0:1, lanes(tile)] * kv[rows, lanes(tile)].astype(F32)
+                hid[rows, lanes(tile)] = (
+                    gate[rows, lanes(tile)].astype(F32) * (part.astype(F32) + direct)
+                ).astype(BF16)
+
+        for to in (yp, ym, zp):
+            gather(half, ten, to)
+
+    def cross(half):
+        arrived(half, zp)
+        gather(half, zp, yp)
+        gather(half, zp, ym)
+
+    def ring(half):
+        arrived(half, ym)
+        arrived(half, yp)
+        gather(half, jnp.where(first_core, ym, yp), ahead)
+
+    def distant(half):
+        arrived(half, far + down)
+        arrived(half, far + up)
+        gather(half, jnp.where(first_core, far + down, far + up), ahead)
+
+    settled(0)
+    settled(1)
+    ring(0)
+    cross(0)
     pushed(node(0, 2))
     spread(2)
-    arrived(zp, every)
-    gather(zp, upper, yp)
-    gather(zp, upper, ym)
-    ahead = jnp.where(first_core, yp, ym)
-    arrived(ym, every)
-    arrived(yp, every)
-    gather(jnp.where(first_core, ym, yp), every, ahead)
-    gather(ym, lower, zp, 1)
-    gather(yp, lower, zp, 1)
+    ring(1)
+    cross(1)
     onward(1)
     onward(3)
+    distant(0)
     onward(2)
-    arrived(far + down, upper)
-    arrived(far + up, upper)
-    gather(jnp.where(first_core, far + down, far + up), upper, ahead)
-    arrived(near + across, every)
-    gather(near + across, lower, zp, 1)
     for dz in range(4):
         pushed(node(2, dz))
         push(node(2, dz), node(0, 0, True)).start()
+    distant(1)
     for dx in range(4):
         for dz in range(4):
             pushed(node(dx, dz, True))
@@ -438,13 +470,12 @@
     project(zp)
     project(ym)
     project(yp)
-    project(near + across)
-    for block in (far + down, far + up):
-        arrived(block, lower, 1)
+    project(far + down)
+    project(far + up)
+    for block in (near + across, far + across):
+        for half in range(2):
+            arrived(half, block)
         project(block)
-    arrived(far + across, upper)
-    arrived(far + across, lower, 1)
-    project(far + across)
     out[...] = acc[...].astype(BF16)
     for c in gathers:
         c.wait_send()
@@ -452,17 +483,11 @@
         c.wait_send()
     settle(xr, xs, xsend, xrecv)
     settle(fr, fs, fsend, frecv)
-    settle(cr, cs, csend, crecv)
+    for half in range(2):
+        settle(cr.at[half], cs.at[half], csend.at[half], crecv.at[half])
 
 
 def body(keyval, gating, skip_gain, filter_values, blocks, out_weight):
-    me = lax.axis_index("seq")
-    groups = blocks.shape[0]
-    match = me * groups // SEQ == jnp.arange(groups, dtype=jnp.int32)
-    kept = jnp.sum(jnp.where(match[:, None], blocks, 0), axis=0)
-    kept = (kept[:, None] * 2 + jnp.arange(2, dtype=jnp.int32)[None, :]).reshape(KEPT)
-    kcol = jnp.broadcast_to(kept[:, None], (KEPT, 128))
-    krow = jnp.broadcast_to(kept[None, :], (8, KEPT))
     vmem = pl.BlockSpec(memory_space=pltpu.VMEM)
     away = pl.BlockSpec(memory_space=pl.ANY)
     dma = pltpu.SemaphoreType.DMA
@@ -473,9 +498,10 @@
     return pl.pallas_call(
         kernel,
         out_shape=jax.ShapeDtypeStruct((TOK, WIDTH), BF16),
-        in_specs=[away, away, vmem, away, vmem, vmem, away],
+        in_specs=[away, away, vmem, away, vmem, away],
         out_specs=vmem,
         scratch_shapes=[
+            buf(KEPT, 128, dtype=jnp.int32), buf(8, KEPT, dtype=jnp.int32),
             buf(TOK, WIDTH), buf(TOK, WIDTH), buf(2048, 128, dtype=F32),
             buf(SEQ, 128, 128), buf(SEQ, 128, 128),
             buf(SEQ, 64, 128), buf(SEQ, 64, 128),
@@ -484,17 +510,17 @@
             buf(4, 512, 128, dtype=F32), buf(512, 256), buf(8, 512, 256, dtype=F32),
             buf(4, 1024, 256), buf(2, 128, 256),
             buf(8, 512, 256), buf(8, 512, 256),
-            buf(SEQ, 128, 128), buf(SEQ, 128, 128), buf(8, TOK, WIDTH),
+            buf(2, SEQ, 64, 128), buf(2, SEQ, 64, 128), buf(8, TOK, WIDTH),
             buf(SEQ, 256, WIDTH), buf(TOK, WIDTH, dtype=F32),
-            dma((SEQ,)), dma((SEQ,)), dma((SEQ,)), dma((SEQ,)), dma((SEQ,)), dma((SEQ,)),
-            dma((10,)), dma((2, 8)), dma((31,)), dma((SEQ,)), dma((4,)),
+            dma((SEQ,)), dma((SEQ,)), dma((SEQ,)), dma((SEQ,)), dma((2, SEQ)), dma((2, SEQ)),
+            dma((14,)), dma((2, 8)), dma((31,)), dma((SEQ,)), dma((4,)),
         ],
         compiler_params=pltpu.CompilerParams(
             collective_id=0, has_side_effects=True, vmem_limit_bytes=60 * 2**20
         ),
     )(
         keyval, gating, skip_gain.reshape(1, WIDTH), filter_values.reshape(2048, 128),
-        kcol, krow, out_weight,
+        blocks, out_weight,
     )
 
 

time: 181 us -> 175 us (0.967)
  Pallas kernels: 176 us -> 171 us
  local copies, waits for them, and re-layouts: 4.39 us -> 2.26 us
    pallas_call x1, Pallas kernels: 176 us -> 171 us  [body(): pl.pallas_call(kernel, out_shape=jax.ShapeDtypeStruct((TOK, WIDTH), BF16)...]
where the time goes in v3:
time: 175 us; the launch traced here: 173 us
  Pallas kernels  171 us (98%)
  local copies, waits for them, and re-layouts  2.26 us (1%)
    pallas_call x1, Pallas kernels, body(): pl.pallas_call(kernel, out_shape=jax.ShapeDtypeStruct((TOK, WIDTH), BF16)...  171 us

profile of v3, /device:TPU:33, one launch (start us, length us, event | category | flops | bytes accessed | tf_op | source)
XLA Modules:
  0.0 173.3 jit_solution(3741607185652834187)
XLA Ops:
  0.0 171.1 %shard_map.64 = bf16[512,1024]{1,0:T(8,128)(2,1)} custom-call(bf16[512,1024]{1,0:T(8,128)(2,1)} %kv_in.1, bf16[512,1024]{1,0:T(8,128)(2,1)} %gate_in.1, f32[1,1024]{1,0:T(1,128)} %bitcast.3, f32[2048,128]{1,0:T(8,128)} %bitcast.2, s32[8,64]{1,0:T(8,128)} %blocks.1, bf16[256,1024]{1,0:T(8,128)(2,1)} %weight_in.1), custom_call_target="tpu_custom_call" | custom-call | tf_op jit(solution)/shard_map/pallas_call | solution.py:498
  171.1 2.3 %copy.8 = bf16[512,1024]{1,0:T(8,128)(2,1)} copy(bf16[512,1024]{1,0:T(8,128)(2,1)} %shard_map.64) | data formatting | bytes 2097152

commit v4 on v3

--- a/solution.py
+++ b/solution.py
@@ -19,6 +19,7 @@
 STEP = 16
 ROWS = TOK // STEP
 HALF = TOK // 2
+UPPER = 176
 LENGTH = SEQ * TOK
 F32 = jnp.float32
 BF16 = jnp.bfloat16
@@ -323,7 +324,6 @@
             fst[p // 2, more, cols] = (im * tc - re * ts).astype(BF16)
 
     collect(fr, fs, fsend, frecv)
-
     @pl.loop(0, OUTER // 2)
     def _(w):
         for half in range(2):
@@ -377,35 +377,31 @@
                     OUTER * l + a, part, cs.at[half], cr.at[half], csend.at[half], crecv.at[half]
                 )
 
+    loads[3].wait()
+
     for dz in (3, 1):
         pushed(node(0, dz))
-    push(
-        jnp.where(first_core, node(0, 3), node(0, 1)),
-        jnp.where(first_core, node(0, 1), node(0, 3)),
-    ).start()
-    spread(1)
-    spread(3)
+        spread(dz)
     onward(0)
-    loads[3].wait()
-
     hid = gath.at[ten]
     gathers = []
-    whole = [slice(HALF * half, HALF * (half + 1)) for half in range(2)]
     ahead = jnp.where(first_core, yp, ym)
 
-    def gather(half, block, to):
-        c = remote(
-            gath.at[block, whole[half]], gath.at[block, whole[half]],
-            gsend.at[len(gathers)], grecv.at[half, block], to, "tensor",
+    def remote_rows(half, part, block, index, to):
+        start, size = ((0, HALF), (0, UPPER), (UPPER, HALF - UPPER))[part]
+        rows = pl.ds(HALF * half + start, size)
+        return remote(
+            gath.at[block, rows], gath.at[block, rows],
+            gsend.at[index], grecv.at[part // 2, half, block], to, "tensor",
         )
+
+    def gather(half, block, to, part=0):
+        c = remote_rows(half, part, block, len(gathers), to)
         gathers.append(c)
         c.start()
 
-    def arrived(half, block):
-        remote(
-            gath.at[block, whole[half]], gath.at[block, whole[half]],
-            gsend.at[0], grecv.at[half, block], zp, "tensor",
-        ).wait_recv()
+    def arrived(half, block, part=0):
+        remote_rows(half, part, block, 0, zp).wait_recv()
 
     def settled(half):
         collect(cr.at[half], cs.at[half], csend.at[half], crecv.at[half])
@@ -425,35 +421,47 @@
 
     def cross(half):
         arrived(half, zp)
-        gather(half, zp, yp)
-        gather(half, zp, ym)
+        gather(half, zp, yp, 1)
+        gather(half, zp, ym, 1)
 
     def ring(half):
         arrived(half, ym)
         arrived(half, yp)
         gather(half, jnp.where(first_core, ym, yp), ahead)
+        gather(half, ym, zp, 2)
+        gather(half, yp, zp, 2)
 
     def distant(half):
-        arrived(half, far + down)
-        arrived(half, far + up)
-        gather(half, jnp.where(first_core, far + down, far + up), ahead)
+        arrived(half, far + down, 1)
+        arrived(half, far + up, 1)
+        gather(half, jnp.where(first_core, far + down, far + up), ahead, 1)
+
+    def closing(half):
+        arrived(half, near + across)
+        gather(half, near + across, zp, 2)
 
     settled(0)
+    push(
+        jnp.where(first_core, node(0, 3), node(0, 1)),
+        jnp.where(first_core, node(0, 1), node(0, 3)),
+    ).start()
     settled(1)
+    onward(3)
+    onward(1)
     ring(0)
     cross(0)
     pushed(node(0, 2))
     spread(2)
     ring(1)
     cross(1)
-    onward(1)
-    onward(3)
+    closing(0)
     distant(0)
     onward(2)
-    for dz in range(4):
+    closing(1)
+    distant(1)
+    for dz in (0, 3, 1, 2):
         pushed(node(2, dz))
         push(node(2, dz), node(0, 0, True)).start()
-    distant(1)
     for dx in range(4):
         for dz in range(4):
             pushed(node(dx, dz, True))
@@ -470,12 +478,15 @@
     project(zp)
     project(ym)
     project(yp)
-    project(far + down)
-    project(far + up)
-    for block in (near + across, far + across):
+    project(near + across)
+    for block in (far + down, far + up):
         for half in range(2):
-            arrived(half, block)
+            arrived(half, block, 2)
         project(block)
+    for half in range(2):
+        arrived(half, far + across, 1)
+        arrived(half, far + across, 2)
+    project(far + across)
     out[...] = acc[...].astype(BF16)
     for c in gathers:
         c.wait_send()
@@ -513,7 +524,7 @@
             buf(2, SEQ, 64, 128), buf(2, SEQ, 64, 128), buf(8, TOK, WIDTH),
             buf(SEQ, 256, WIDTH), buf(TOK, WIDTH, dtype=F32),
             dma((SEQ,)), dma((SEQ,)), dma((SEQ,)), dma((SEQ,)), dma((2, SEQ)), dma((2, SEQ)),
-            dma((14,)), dma((2, 8)), dma((31,)), dma((SEQ,)), dma((4,)),
+            dma((20,)), dma((2, 2, 8)), dma((31,)), dma((SEQ,)), dma((4,)),
         ],
         compiler_params=pltpu.CompilerParams(
             collective_id=0, has_side_effects=True, vmem_limit_bytes=60 * 2**20

time: 175 us -> 168 us (0.960)
  Pallas kernels: 171 us -> 166 us
    pallas_call x1, Pallas kernels: 171 us -> 166 us  [body(): pl.pallas_call(kernel, out_shape=jax.ShapeDtypeStruct((TOK, WIDTH), BF16)...]
where the time goes in v4:
time: 168 us
  Pallas kernels  166 us (99%)
  local copies, waits for them, and re-layouts  2.26 us (1%)
    pallas_call x1, Pallas kernels, body(): pl.pallas_call(kernel, out_shape=jax.ShapeDtypeStruct((TOK, WIDTH), BF16)...  166 us

profile of v4, /device:TPU:33, one launch (start us, length us, event | category | flops | bytes accessed | tf_op | source)
XLA Modules:
  0.0 167.9 jit_solution(5963924687569842694)
XLA Ops:
  0.0 165.6 %shard_map.64 = bf16[512,1024]{1,0:T(8,128)(2,1)} custom-call(bf16[512,1024]{1,0:T(8,128)(2,1)} %kv_in.1, bf16[512,1024]{1,0:T(8,128)(2,1)} %gate_in.1, f32[1,1024]{1,0:T(1,128)} %bitcast.3, f32[2048,128]{1,0:T(8,128)} %bitcast.2, s32[8,64]{1,0:T(8,128)} %blocks.1, bf16[256,1024]{1,0:T(8,128)(2,1)} %weight_in.1), custom_call_target="tpu_custom_call" | custom-call | tf_op jit(solution)/shard_map/pallas_call | solution.py:509
  165.6 2.3 %copy.8 = bf16[512,1024]{1,0:T(8,128)(2,1)} copy(bf16[512,1024]{1,0:T(8,128)(2,1)} %shard_map.64) | data formatting | bytes 2097152

commit v5 on v4

--- a/solution.py
+++ b/solution.py
@@ -18,8 +18,13 @@
 KEPT = 128
 STEP = 16
 ROWS = TOK // STEP
-HALF = TOK // 2
-UPPER = 176
+HALF = WIDTH // 2
+UPPER = 448
+WZ = 3
+SEC = 2
+RL = 1
+E2 = 1
+ORDER = "sawbxycdefzghivj"
 LENGTH = SEQ * TOK
 F32 = jnp.float32
 BF16 = jnp.bfloat16
@@ -191,35 +196,46 @@
         block = jnp.where(first_core, node(3, dz), node(1, dz))
         push(block, jnp.where(first_core, node(1, 0), node(3, 0))).start()
 
+    def begin():
+        for dz in (1, 3):
+            push(me, node(0, dz)).start()
+
     loads[0].wait()
     pl.semaphore_wait(barrier, SEQ - 1 + 3)
 
-    @pl.loop(0, OUTER)
-    def _(i):
-        tile = lax.rem(me // INNER + i, OUTER)
-        parts = [kv[QUARTER * k : QUARTER * (k + 1), lanes(tile)] for k in range(INNER)]
-        for q, part in enumerate(swap(parts, perm)):
-            deliver(tile * INNER + q, part, xs, xr, xsend, xrecv)
-
-    loads[2].wait()
-
-    @pl.loop(0, OUTER)
-    def _(i):
-        tile = lax.rem(me // INNER + i, OUTER)
-        parts = []
-        for k in range(INNER):
-            pair = [
-                filt[pl.ds(m * 1024 + 256 * k + tile, UNIT, stride=8), :].astype(BF16)
-                for m in range(2)
-            ]
-            parts.append(jnp.concatenate(pair, axis=0))
-        for q, part in enumerate(swap(parts, perm)):
-            deliver(tile * INNER + q, part, fs, fr, fsend, frecv)
+    for phase in range(2):
+
+        @pl.loop(0, INNER)
+        def _(i):
+            plane = lax.rem(x + i, INNER)
+            tile = INNER * phase + plane
+            parts = [kv[QUARTER * k : QUARTER * (k + 1), lanes(tile)] for k in range(INNER)]
+            for q, part in enumerate(swap(parts, perm)):
+                deliver(plane * 8 + 2 * q + phase, part, xs, xr, xsend, xrecv)
+
+        if phase == 0:
+            loads[2].wait()
+
+        @pl.loop(0, INNER)
+        def _(i):
+            plane = lax.rem(x + i, INNER)
+            tile = INNER * phase + plane
+            parts = []
+            for k in range(INNER):
+                pair = [
+                    filt[pl.ds(m * 1024 + 256 * k + tile, UNIT, stride=8), :].astype(BF16)
+                    for m in range(2)
+                ]
+                parts.append(jnp.concatenate(pair, axis=0))
+            for q, part in enumerate(swap(parts, perm)):
+                deliver(plane * 8 + 2 * q + phase, part, fs, fr, fsend, frecv)
 
     loads[1].wait()
     spread(0)
-
-    group = iota((OUTER, 64), 0) == me // INNER
+    if WZ == 3:
+        begin()
+
+    group = iota((OUTER, 64), 0) == INNER * core + x
     listed = jnp.sum(jnp.where(group, blocks[...].astype(F32), 0.0), axis=0, keepdims=True)
     own = iota((KEPT, 64), 1) == (iota((KEPT, 64), 0) >> 1)
     column = jnp.sum(jnp.where(own, listed, 0.0), axis=1, keepdims=True)
@@ -293,8 +309,8 @@
         tw[3, rows, :] = sine(beta)
 
     collect(xr, xs, xsend, xrecv)
-    for dz in (1, 3):
-        push(me, node(0, dz)).start()
+    if WZ == 2:
+        begin()
 
     @pl.loop(0, OUTER)
     def _(a):
@@ -341,57 +357,48 @@
             rows = slice(TOK * part, TOK * (part + 1))
             g[2 * w + part] = dot(th[rows], hi) + dot(tl[rows], hi) + dot(th[rows], lo)
 
-    for half in range(2):
-
-        @pl.loop(half * (ROWS // 2), (half + 1) * (ROWS // 2))
-        def _(r):
-            rows = pl.ds(pl.multiple_of(r * STEP, STEP), STEP)
-            turned = []
-            for p, (tc, ts) in enumerate(twists(rows)):
-                cols = slice(128 * (p % 2), 128 * (p % 2) + 128)
-                re, im = g[p // 2 * 2, rows, cols], g[p // 2 * 2 + 1, rows, cols]
-                turned.append(
-                    (
-                        (re * tc - im * ts).astype(BF16).astype(F32),
-                        (re * ts + im * tc).astype(BF16).astype(F32),
-                    )
+    @pl.loop(0, ROWS)
+    def _(r):
+        rows = pl.ds(pl.multiple_of(r * STEP, STEP), STEP)
+        turned = []
+        for p, (tc, ts) in enumerate(twists(rows)):
+            cols = slice(128 * (p % 2), 128 * (p % 2) + 128)
+            re, im = g[p // 2 * 2, rows, cols], g[p // 2 * 2 + 1, rows, cols]
+            turned.append(
+                (
+                    (re * tc - im * ts).astype(BF16).astype(F32),
+                    (re * ts + im * tc).astype(BF16).astype(F32),
                 )
-            for a, (re, im) in enumerate(transform(turned, 1)):
-                hi, lo = halves(re)
-                vh[a, rows, 0:128] = hi
-                vl[a, rows, 0:128] = lo
-                hi, lo = halves(im)
-                vh[a, rows, 128:256] = hi
-                vl[a, rows, 128:256] = lo
-
-        @pl.loop(0, OUTER)
-        def _(i):
-            a = lax.rem(lax.rem(me, OUTER) + i, OUTER)
-            rows = slice(HALF * half, HALF * (half + 1))
-            v, rest = vh[a, rows], vl[a, rows]
-            c = dot(v, eh[a]) + dot(rest, eh[a]) + dot(v, el[a])
-            c = (c * (1.0 / LENGTH)).astype(BF16)
-            parts = [c[64 * k : 64 * (k + 1)] for k in range(INNER)]
-            for l, part in enumerate(swap(parts, perm)):
-                deliver(
-                    OUTER * l + a, part, cs.at[half], cr.at[half], csend.at[half], crecv.at[half]
-                )
-
+            )
+        for a, (re, im) in enumerate(transform(turned, 1)):
+            hi, lo = halves(re)
+            vh[a, rows, 0:128] = hi
+            vl[a, rows, 0:128] = lo
+            hi, lo = halves(im)
+            vh[a, rows, 128:256] = hi
+            vl[a, rows, 128:256] = lo
+
+    @pl.loop(0, OUTER)
+    def _(i):
+        a = lax.rem(lax.rem(me, OUTER) + i, OUTER)
+        c = dot(vh[a], eh[a]) + dot(vl[a], eh[a]) + dot(vh[a], el[a])
+        c = (c * (1.0 / LENGTH)).astype(BF16)
+        parts = [c[QUARTER * k : QUARTER * (k + 1)] for k in range(INNER)]
+        for l, part in enumerate(swap(parts, perm)):
+            deliver(OUTER * l + a, part, cs, cr, csend, crecv)
+
+    if WZ == 0:
+        begin()
     loads[3].wait()
 
-    for dz in (3, 1):
-        pushed(node(0, dz))
-        spread(dz)
-    onward(0)
-    hid = gath.at[ten]
     gathers = []
     ahead = jnp.where(first_core, yp, ym)
 
     def remote_rows(half, part, block, index, to):
-        start, size = ((0, HALF), (0, UPPER), (UPPER, HALF - UPPER))[part]
-        rows = pl.ds(HALF * half + start, size)
+        start, size = ((0, TOK), (0, UPPER), (UPPER, TOK - UPPER))[part]
+        rows = pl.ds(start, size)
         return remote(
-            gath.at[block, rows], gath.at[block, rows],
+            gath.at[block, half, rows], gath.at[block, half, rows],
             gsend.at[index], grecv.at[part // 2, half, block], to, "tensor",
         )
 
@@ -404,15 +411,22 @@
         remote_rows(half, part, block, 0, zp).wait_recv()
 
     def settled(half):
-        collect(cr.at[half], cs.at[half], csend.at[half], crecv.at[half])
-
-        @pl.loop(0, OUTER)
-        def _(tile):
-            parts = [cr[half, INNER * tile + q] for q in range(INNER)]
+        @pl.loop(0, SEQ // 2)
+        def _(i):
+            src = 2 * i + half
+
+            @pl.when(src != me)
+            def _():
+                remote(cs.at[src], cr.at[src], csend.at[src], crecv.at[src], src).wait_recv()
+
+        @pl.loop(0, INNER)
+        def _(plane):
+            tile = INNER * half + plane
+            parts = [cr[plane * 8 + 2 * q + half] for q in range(INNER)]
             for k, part in enumerate(swap(parts, perm)):
-                rows = slice(HALF * half + 64 * k, HALF * half + 64 * (k + 1))
+                rows = slice(QUARTER * k, QUARTER * (k + 1))
                 direct = skip[0:1, lanes(tile)] * kv[rows, lanes(tile)].astype(F32)
-                hid[rows, lanes(tile)] = (
+                gath[ten, half, rows, lanes(plane)] = (
                     gate[rows, lanes(tile)].astype(F32) * (part.astype(F32) + direct)
                 ).astype(BF16)
 
@@ -440,28 +454,38 @@
         arrived(half, near + across)
         gather(half, near + across, zp, 2)
 
-    settled(0)
-    push(
-        jnp.where(first_core, node(0, 3), node(0, 1)),
-        jnp.where(first_core, node(0, 1), node(0, 3)),
-    ).start()
-    settled(1)
-    onward(3)
-    onward(1)
-    ring(0)
-    cross(0)
-    pushed(node(0, 2))
-    spread(2)
-    ring(1)
-    cross(1)
-    closing(0)
-    distant(0)
-    onward(2)
-    closing(1)
-    distant(1)
-    for dz in (0, 3, 1, 2):
-        pushed(node(2, dz))
-        push(node(2, dz), node(0, 0, True)).start()
+    def forward():
+        push(
+            jnp.where(first_core, node(0, 3), node(0, 1)),
+            jnp.where(first_core, node(0, 1), node(0, 3)),
+        ).start()
+
+    def second():
+        for dz in (3, 1):
+            pushed(node(0, dz))
+            spread(dz)
+        if RL == 1:
+            forward()
+        onward(0)
+
+    def early():
+        pushed(node(0, 2))
+        spread(2)
+
+    def last():
+        for dz in (0, 3, 1, 2):
+            pushed(node(2, dz))
+            push(node(2, dz), node(0, 0, True)).start()
+
+    steps = dict(
+        a=lambda: settled(0), b=lambda: settled(1), c=lambda: ring(0), d=lambda: cross(0),
+        e=lambda: ring(1), f=lambda: cross(1), g=lambda: closing(0), h=lambda: distant(0),
+        i=lambda: closing(1), j=lambda: distant(1), w=lambda: early(), x=lambda: onward(3),
+        y=lambda: onward(1), z=lambda: onward(2), v=lambda: last(), s=lambda: second(),
+    )
+    for key in ORDER:
+        steps[key]()
+
     for dx in range(4):
         for dz in range(4):
             pushed(node(dx, dz, True))
@@ -470,8 +494,9 @@
         @pl.loop(0, 4)
         def _(n):
             cols = pl.ds(pl.multiple_of(n * 256, 256), 256)
-            w = wv[pl.ds(INNER * block, INNER), :, cols].reshape(WIDTH, 256)
-            part = dot(gath[block], w)
+            low = wv[pl.ds(INNER * block, 2), :, cols].reshape(HALF, 256)
+            high = wv[pl.ds(INNER * block + 2, 2), :, cols].reshape(HALF, 256)
+            part = dot(gath[block, 0], low) + dot(gath[block, 1], high)
             acc[:, cols] = part if start else acc[:, cols] + part
 
     project(ten, True)
@@ -494,8 +519,7 @@
         c.wait_send()
     settle(xr, xs, xsend, xrecv)
     settle(fr, fs, fsend, frecv)
-    for half in range(2):
-        settle(cr.at[half], cs.at[half], csend.at[half], crecv.at[half])
+    settle(cr, cs, csend, crecv)
 
 
 def body(keyval, gating, skip_gain, filter_values, blocks, out_weight):
@@ -521,9 +545,9 @@
             buf(4, 512, 128, dtype=F32), buf(512, 256), buf(8, 512, 256, dtype=F32),
             buf(4, 1024, 256), buf(2, 128, 256),
             buf(8, 512, 256), buf(8, 512, 256),
-            buf(2, SEQ, 64, 128), buf(2, SEQ, 64, 128), buf(8, TOK, WIDTH),
+            buf(SEQ, 128, 128), buf(SEQ, 128, 128), buf(8, 2, TOK, HALF),
             buf(SEQ, 256, WIDTH), buf(TOK, WIDTH, dtype=F32),
-            dma((SEQ,)), dma((SEQ,)), dma((SEQ,)), dma((SEQ,)), dma((2, SEQ)), dma((2, SEQ)),
+            dma((SEQ,)), dma((SEQ,)), dma((SEQ,)), dma((SEQ,)), dma((SEQ,)), dma((SEQ,)),
             dma((20,)), dma((2, 2, 8)), dma((31,)), dma((SEQ,)), dma((4,)),
         ],
         compiler_params=pltpu.CompilerParams(

time: 168 us -> 173 us (1.030); the launches traced: 168 us -> 170 us
  Pallas kernels: 166 us -> 168 us
    pallas_call x1, Pallas kernels: 166 us -> 168 us  [body(): pl.pallas_call(kernel, out_shape=jax.ShapeDtypeStruct((TOK, WIDTH), BF16)...]
where the time goes in v5:
time: 173 us; the launch traced here: 170 us
  Pallas kernels  168 us (97%)
  local copies, waits for them, and re-layouts  2.26 us (1%)
    pallas_call x1, Pallas kernels, body(): pl.pallas_call(kernel, out_shape=jax.ShapeDtypeStruct((TOK, WIDTH), BF16)...  168 us

profile of v5, /device:TPU:33, one launch (start us, length us, event | category | flops | bytes accessed | tf_op | source)
XLA Modules:
  0.0 170.1 jit_solution(12867869954973022308)
XLA Ops:
  0.0 167.8 %shard_map.64 = bf16[512,1024]{1,0:T(8,128)(2,1)} custom-call(bf16[512,1024]{1,0:T(8,128)(2,1)} %kv_in.1, bf16[512,1024]{1,0:T(8,128)(2,1)} %gate_in.1, f32[1,1024]{1,0:T(1,128)} %bitcast.3, f32[2048,128]{1,0:T(8,128)} %bitcast.2, s32[8,64]{1,0:T(8,128)} %blocks.1, bf16[256,1024]{1,0:T(8,128)(2,1)} %weight_in.1), custom_call_target="tpu_custom_call" | custom-call | tf_op jit(solution)/shard_map/pallas_call | solution.py:533
  167.8 2.3 %copy.8 = bf16[512,1024]{1,0:T(8,128)(2,1)} copy(bf16[512,1024]{1,0:T(8,128)(2,1)} %shard_map.64) | data formatting | bytes 2097152
